TPU v7x, 32 devices: a whole 2x2x4 slice. The times are simulated.
32 devices in a mesh: occ: 8 (over y, x, core), ao: 4 (over z).
Axes of the slice: x: 2, y: 2, z: 4, core: 2. Of those that a mesh axis runs over, the one named last changes fastest.
Arguments:
- coef: bfloat16 [2048, 8], P('ao', 'occ'), may hold values from -0.5 to 0.5
- half_ints: bfloat16 [8, 1024, 2048], P('occ', None, 'ao'), may hold values from -0.5 to 0.5
- metric_inv: bfloat16 [64, 128, 128], replicated, may hold values from -1 to 2, as said below
- dom_blocks: int32 [8, 8], P('occ'), may hold values from 0 to 63, as said below
- dom_len: int32 [8], P('occ'), may hold values from 2 to 8
Outputs:
- exchange_k: float32 [2048, 2048], P('ao', 'occ')
- fit_density: float32 [8192], replicated
Inputs may be any that keep to these rules, and one draw needn't show every extreme that they name: `dom_blocks`: each row holds 8 different block numbers. `metric_inv`: full rank blocks.
All inputs are finite; a program needn't handle non-finite values.
Results may differ from a plain program's by a relative error of at most 0.0055.
Values may be sent and summed in bfloat16 or wider, within the bound.
No kernel may reach another device: no remote copies, remote signals or barrier semaphores. Data moves between devices by JAX's collectives and lax.ppermute only.
A program may use at most 128 MiB of HBM per device.

v0:
```python
import jax
import jax.numpy as jnp
from jax import lax
from jax.sharding import PartitionSpec as P


def on_device(coef, half_ints, metric_inv, dom_blocks, dom_len):
    lmo_count, domain, ao_rows = half_ints.shape
    block = metric_inv.shape[1]
    slots = domain // block
    fit_blocks = metric_inv.shape[0]
    metric_rows = metric_inv[dom_blocks]
    raw_ints = half_ints.reshape(lmo_count, slots, block, ao_rows)
    fitted = jnp.einsum(
        "isab,isbm->isam", metric_rows, raw_ints, preferred_element_type=jnp.float32
    )
    live_slots = jnp.arange(slots, dtype=jnp.int32)[None, :] < dom_len[:, None]
    fitted = jnp.where(live_slots[:, :, None, None], fitted, 0.0)
    fitted = fitted.reshape(lmo_count, domain, ao_rows).astype(jnp.bfloat16)
    pair_part = jnp.einsum("ipm,mi->ip", fitted, coef, preferred_element_type=jnp.float32)
    one_hot = (
        dom_blocks[:, :, None] == jnp.arange(fit_blocks, dtype=jnp.int32)[None, None, :]
    ).astype(jnp.float32)
    local_density = jnp.einsum("isf,isr->fr", one_hot, pair_part.reshape(lmo_count, slots, block))
    density = lax.psum(local_density, ("occ", "ao"))
    density = density.reshape(fit_blocks * block)
    partial_value = jnp.einsum(
        "ipm,ipn->mn",
        fitted,
        lax.all_gather(fitted, "ao", axis=2, tiled=True),
        preferred_element_type=jnp.float32,
    )
    exchange_k = lax.psum_scatter(partial_value, "occ", scatter_dimension=1, tiled=True)
    return (exchange_k, density)


def solution(mesh):
    in_specs = (P("ao", "occ"), P("occ", None, "ao"), P(), P("occ", None), P("occ"))
    out_specs = (P("ao", "occ"), P())
    return jax.shard_map(
        on_device, mesh=mesh, in_specs=in_specs, out_specs=out_specs, check_vma=False
    )
```

profile of v0, /device:TPU:0, one launch (start us, length us, event | category | flops | bytes accessed | tf_op | source)
XLA Modules:
  0.0 159.3 jit_solution(12443113816982479165)
XLA Ops:
  7.2 0.0 copy-start
  7.2 0.0 all-gather.2.cloned.1.call-start
  8.0 0.7 fusion.5
  8.7 0.1 copy-done
  8.8 0.6 gather_fusion
  9.4 2.7 %select_convert_fusion = bf16[8,128,512]{2,1,0:T(8,128)(2,1)} fusion(bf16[8,128,128]{2,1,0:T(8,128)(2,1)S(1)} %gather_fusion, bf16[8,128,512]{2,1,0:T(8,128)(2,1)} %bitcast.25, pred[8]{0:T(512)(128)(4,1)S(1)} %iota_compare_fusion.2), kind=kOutput, calls=%fused_computation.3 | convolution fusion | flops 135266304 | bytes 2359304 | tf_op jit(solution)/shard_map/isab,isbm->isam/dot_general | solution.py:14
  12.1 0.0 all-gather.2.cloned.1.call-update
  12.1 0.0 reduce-scatter.2.cloned.1.call-start
  12.1 83.6 %all-gather.2.cloned.1.call-done = bf16[1,1024,2048]{2,1,0:T(8,128)(2,1)} async-done(((bf16[1,1024,512]{2,1,0:T(8,128)(2,1)}), bf16[1,1024,2048]{2,1,0:T(8,128)(2,1)}) %all-gather.2.cloned.1.call-update) | async-done | bytes 4194320 | tf_op jit(solution)/shard_map/all_gather | solution.py:30
  95.7 6.8 %fusion = f32[512,2048]{1,0:T(8,128)} fusion(bf16[1024,512]{1,0:T(8,128)(2,1)} %bitcast.24, bf16[1,1024,2048]{2,1,0:T(8,128)(2,1)} %all-gather.2.cloned.1.call-done), kind=kOutput, calls=%fused_computation.1 | convolution fusion | flops 2147483648 | bytes 9437184 | tf_op jit(solution)/shard_map/ipm,ipn->mn/dot_general | solution.py:27
  102.5 0.0 copy-start.1
  102.5 0.0 copy-start.2
  102.5 0.0 copy-start.3
  102.5 0.0 reduce-scatter.2.cloned.1.call-update
  102.6 1.2 copy-done.1
  103.8 0.0 copy-done.2
  103.8 0.4 fusion.2
  104.1 0.0 copy-done.3
  104.1 0.3 convolution_bitcast_fusion
  104.4 39.3 %psum.7 = f32[8192]{0:T(1024)} all-reduce(f32[8192]{0:T(1024)S(1)} %convolution_bitcast_fusion), channel_id=1, replica_groups=mesh['occ'=8,'ao'=4] {'occ','ao'}, use_global_device_ids=true, to_apply=%region_1.2 | all-reduce | flops 8192 | bytes 65536 | tf_op jit(solution)/shard_map/psum | solution.py:25
  143.7 8.8 %reduce-scatter.2.cloned.1.call-done = f32[512,256]{1,0:T(8,128)} async-done(((f32[512,2048]{1,0:T(8,128)}), f32[512,256]{1,0:T(8,128)}) %reduce-scatter.2.cloned.1.call-update) | async-done | bytes 524304 | tf_op jit(solution)/shard_map/reduce_scatter | solution.py:33
  (2 shorter events, 0.0 us)
Async XLA Ops:
  7.2 1.6 %copy-start = (bf16[64,128,128]{2,1,0:T(8,128)(2,1)S(1)}, bf16[64,128,128]{2,1,0:T(8,128)(2,1)}, u32[]{:S(2)}) copy-start(bf16[64,128,128]{2,1,0:T(8,128)(2,1)} %param.7) | copy-start | bytes 6291460
  7.2 88.5 %all-gather.2.cloned.1.call-start = ((), (), s32[]{:S(2)}) async-start(), calls=%async_computation.1 | async-start | bytes 5242880 | tf_op jit(solution)/shard_map/all_gather | solution.py:30
  12.1 140.4 %reduce-scatter.2.cloned.1.call-start = ((), (), s32[]{:S(2)}) async-start(), calls=%async_computation.2 | async-start | bytes 4718592 | tf_op jit(solution)/shard_map/reduce_scatter | solution.py:33
  102.5 1.2 copy-start.1
  102.5 1.2 copy-start.2
  102.5 1.6 copy-start.3
Sparse Core Ops, SparseCore 0:
  12.2 83.4 all-gather.1
  102.7 49.7 reduce-scatter.1
where the time goes:
time: 160 us; the launch traced here: 159 us
  waiting for transfers between devices  92.3 us (58%)
  blocking collectives  39.3 us (25%)
  between operations  14.8 us (9%)
  matrix products  10.2 us (6%)
  local copies, waits for them, and re-layouts  1.89 us (1%)
    all_gather x1, waiting for transfers between devices, on_device(): lax.all_gather(fitted, 'ao', axis=2, tiled=True)  83.6 us
    psum x1, blocking collectives, on_device(): density = lax.psum(local_density, ('occ', 'ao'))  39.3 us
    reduce_scatter x1, waiting for transfers between devices, on_device(): lax.psum_scatter(partial_value, 'occ', scatter_dimension=1, tiled=True)  8.75 us
    dot_general x1, matrix products, on_device(): jnp.einsum('ipm,ipn->mn', fitted, lax.all_gather(fitted, 'ao', axis=2, ti...  6.82 us
  transfers between devices with their start and end apart: 2, of which 2 were waited for; matrix products, arithmetic and copies ran while one was open for 0% of the time, Pallas kernels for 0%

commit v1 on v0

--- a/solution.py
+++ b/solution.py
@@ -22,7 +22,7 @@
         dom_blocks[:, :, None] == jnp.arange(fit_blocks, dtype=jnp.int32)[None, None, :]
     ).astype(jnp.float32)
     local_density = jnp.einsum("isf,isr->fr", one_hot, pair_part.reshape(lmo_count, slots, block))
-    density = lax.psum(local_density, ("occ", "ao"))
+    density = jnp.sum(lax.all_gather(local_density, ("occ", "ao")), axis=0)
     density = density.reshape(fit_blocks * block)
     partial_value = jnp.einsum(
         "ipm,ipn->mn",

time: 160 us -> 212 us (1.32)
  waiting for transfers between devices: 92.3 us -> 182 us
  blocking collectives: 39.3 us -> 0 us
    all_gather x0 -> x1, waiting for transfers between devices: none -> 49 us  [on_device(): density = jnp.sum(lax.all_gather(local_density, ('occ', 'ao')), axis=0)]
    reduce_scatter x1, waiting for transfers between devices: 8.75 us -> 52.1 us  [on_device(): lax.psum_scatter(partial_value, 'occ', scatter_dimension=1, tiled=True)]
    psum x1 -> x0, blocking collectives: 39.3 us -> none  [on_device(): density = lax.psum(local_density, ('occ', 'ao'))]
    all_gather x1, waiting for transfers between devices: 83.6 us -> 81 us  [on_device(): lax.all_gather(fitted, 'ao', axis=2, tiled=True)]
  transfers between devices with their start and end apart: 2 -> 3, of which waited for: 2 -> 3; matrix products, arithmetic and copies ran while one was open for 0% -> 5% of each run, Pallas kernels for 0% -> 0%
where the time goes in v1:
time: 212 us
  waiting for transfers between devices  182 us (86%)
  between operations  14.6 us (7%)
  matrix products  12 us (6%)
  other arithmetic  2.58 us (1%)
    all_gather x1, waiting for transfers between devices, on_device(): lax.all_gather(fitted, 'ao', axis=2, tiled=True)  81 us
    reduce_scatter x1, waiting for transfers between devices, on_device(): lax.psum_scatter(partial_value, 'occ', scatter_dimension=1, tiled=True)  52.1 us
    all_gather x1, waiting for transfers between devices, on_device(): density = jnp.sum(lax.all_gather(local_density, ('occ', 'ao')), axis=0)  49 us
    dot_general x1, matrix products, on_device(): jnp.einsum('ipm,ipn->mn', fitted, lax.all_gather(fitted, 'ao', axis=2, ti...  6.86 us
  transfers between devices with their start and end apart: 3, of which 3 were waited for; matrix products, arithmetic and copies ran while one was open for 5% of the time, Pallas kernels for 0%

profile of v1, /device:TPU:0, one launch (start us, length us, event | category | flops | bytes accessed | tf_op | source)
XLA Modules:
  0.0 212.0 jit_solution(1869800519201846238)
XLA Ops:
  7.2 0.0 copy-start
  7.2 0.0 copy-start.1
  7.2 0.0 all-gather.4.cloned.1.call-start
  8.0 0.7 fusion.6
  8.7 0.1 copy-done
  8.8 0.6 gather_fusion
  9.4 2.6 %select_convert_fusion = bf16[8,128,512]{2,1,0:T(8,128)(2,1)} fusion(bf16[8,128,128]{2,1,0:T(8,128)(2,1)S(1)} %gather_fusion, bf16[8,128,512]{2,1,0:T(8,128)(2,1)} %bitcast.25, pred[8]{0:T(512)(128)(4,1)S(1)} %iota_compare_fusion.2), kind=kOutput, calls=%fused_computation.3 | convolution fusion | flops 135266304 | bytes 2359304 | tf_op jit(solution)/shard_map/isab,isbm->isam/dot_general | solution.py:14
  12.0 0.0 all-gather.4.cloned.1.call-update
  12.0 0.0 all-gather.6.cloned.1.call-start
  12.1 1.6 fusion.3
  13.7 0.0 copy-done.1
  13.7 0.9 fusion.2
  14.6 0.0 all-gather.6.cloned.1.call-update
  14.6 0.0 reduce-scatter.2.cloned.1.call-start
  14.6 81.0 %all-gather.4.cloned.1.call-done = bf16[1,1024,2048]{2,1,0:T(8,128)(2,1)} async-done(((bf16[1,1024,512]{2,1,0:T(8,128)(2,1)}), bf16[1,1024,2048]{2,1,0:T(8,128)(2,1)}) %all-gather.4.cloned.1.call-update) | async-done | bytes 4194320 | tf_op jit(solution)/shard_map/all_gather | solution.py:30
  95.6 6.9 %fusion = f32[512,2048]{1,0:T(8,128)} fusion(bf16[1024,512]{1,0:T(8,128)(2,1)} %bitcast.24, bf16[1,1024,2048]{2,1,0:T(8,128)(2,1)} %all-gather.4.cloned.1.call-done), kind=kOutput, calls=%fused_computation.1 | convolution fusion | flops 2147483648 | bytes 9437184 | tf_op jit(solution)/shard_map/ipm,ipn->mn/dot_general | solution.py:27
  102.5 0.0 reduce-scatter.2.cloned.1.call-update
  102.5 49.0 %all-gather.6.cloned.1.call-done = f32[2048,128]{1,0:T(8,128)} async-done(((f32[64,128]{1,0:T(8,128)}), f32[2048,128]{1,0:T(8,128)}) %all-gather.6.cloned.1.call-update) | async-done | bytes 1048592 | tf_op jit(solution)/shard_map/all_gather | solution.py:25
  151.5 1.9 reduce_sum.9
  153.4 52.1 %reduce-scatter.2.cloned.1.call-done = f32[512,256]{1,0:T(8,128)} async-done(((f32[512,2048]{1,0:T(8,128)}), f32[512,256]{1,0:T(8,128)}) %reduce-scatter.2.cloned.1.call-update) | async-done | bytes 524304 | tf_op jit(solution)/shard_map/reduce_scatter | solution.py:33
  (2 shorter events, 0.0 us)
Async XLA Ops:
  7.2 1.6 copy-start
  7.2 6.5 %copy-start.1 = (s32[1,8]{1,0:T(1,128)S(1)}, s32[1,8]{1,0:T(1,128)}, u32[]{:S(2)}) copy-start(s32[1,8]{1,0:T(1,128)} %param.8) | copy-start | bytes 100
  7.2 88.4 %all-gather.4.cloned.1.call-start = ((), (), s32[]{:S(2)}) async-start(), calls=%async_computation.1 | async-start | bytes 5242880 | tf_op jit(solution)/shard_map/all_gather | solution.py:30
  12.0 139.5 %all-gather.6.cloned.1.call-start = ((), (), s32[]{:S(2)}) async-start(), calls=%async_computation.3 | async-start | bytes 1081344 | tf_op jit(solution)/shard_map/all_gather | solution.py:25
  14.6 190.9 %reduce-scatter.2.cloned.1.call-start = ((), (), s32[]{:S(2)}) async-start(), calls=%async_computation.2 | async-start | bytes 4718592 | tf_op jit(solution)/shard_map/reduce_scatter | solution.py:33
Sparse Core Ops, SparseCore 0:
  12.1 83.4 all-gather.3
  99.2 52.2 all-gather.5
  155.4 50.0 reduce-scatter.1

commit v2 on v0

--- a/solution.py
+++ b/solution.py
@@ -22,7 +22,7 @@
         dom_blocks[:, :, None] == jnp.arange(fit_blocks, dtype=jnp.int32)[None, None, :]
     ).astype(jnp.float32)
     local_density = jnp.einsum("isf,isr->fr", one_hot, pair_part.reshape(lmo_count, slots, block))
-    density = lax.psum(local_density, ("occ", "ao"))
+    density = lax.psum(lax.psum(local_density, "ao"), "occ")
     density = density.reshape(fit_blocks * block)
     partial_value = jnp.einsum(
         "ipm,ipn->mn",

time: 160 us -> 160 us (level)
    psum x1 -> x2, blocking collectives: 39.3 us -> 40.2 us  [on_device(): density = lax.psum(lax.psum(local_density, 'ao'), 'occ')]
where the time goes in v2:
time: 160 us; the launch traced here: 159 us
  waiting for transfers between devices  91.7 us (57%)
  blocking collectives  40.2 us (25%)
  between operations  14.9 us (9%)
  matrix products  10.2 us (6%)
  local copies, waits for them, and re-layouts  1.89 us (1%)
    all_gather x1, waiting for transfers between devices, on_device(): lax.all_gather(fitted, 'ao', axis=2, tiled=True)  83.6 us
    psum x2, blocking collectives, on_device(): density = lax.psum(lax.psum(local_density, 'ao'), 'occ')  40.2 us
    reduce_scatter x1, waiting for transfers between devices, on_device(): lax.psum_scatter(partial_value, 'occ', scatter_dimension=1, tiled=True)  8.08 us
    dot_general x1, matrix products, on_device(): jnp.einsum('ipm,ipn->mn', fitted, lax.all_gather(fitted, 'ao', axis=2, ti...  6.82 us
  transfers between devices with their start and end apart: 2, of which 2 were waited for; matrix products, arithmetic and copies ran while one was open for 0% of the time, Pallas kernels for 0%

profile of v2, /device:TPU:0, one launch (start us, length us, event | category | flops | bytes accessed | tf_op | source)
XLA Modules:
  0.0 159.5 jit_solution(2553503244912495583)
XLA Ops:
  7.2 0.0 copy-start
  7.2 0.0 all-gather.2.cloned.1.call-start
  8.0 0.7 fusion.6
  8.7 0.1 copy-done
  8.8 0.6 gather_fusion
  9.4 2.7 %select_convert_fusion = bf16[8,128,512]{2,1,0:T(8,128)(2,1)} fusion(bf16[8,128,128]{2,1,0:T(8,128)(2,1)S(1)} %gather_fusion, bf16[8,128,512]{2,1,0:T(8,128)(2,1)} %bitcast.24, pred[8]{0:T(512)(128)(4,1)S(1)} %iota_compare_fusion.2), kind=kOutput, calls=%fused_computation.3 | convolution fusion | flops 135266304 | bytes 2359304 | tf_op jit(solution)/shard_map/isab,isbm->isam/dot_general | solution.py:14
  12.1 0.0 all-gather.2.cloned.1.call-update
  12.1 0.0 reduce-scatter.2.cloned.1.call-start
  12.2 83.6 %all-gather.2.cloned.1.call-done = bf16[1,1024,2048]{2,1,0:T(8,128)(2,1)} async-done(((bf16[1,1024,512]{2,1,0:T(8,128)(2,1)}), bf16[1,1024,2048]{2,1,0:T(8,128)(2,1)}) %all-gather.2.cloned.1.call-update) | async-done | bytes 4194320 | tf_op jit(solution)/shard_map/all_gather | solution.py:30
  95.7 6.8 %fusion = f32[512,2048]{1,0:T(8,128)} fusion(bf16[1024,512]{1,0:T(8,128)(2,1)} %bitcast.23, bf16[1,1024,2048]{2,1,0:T(8,128)(2,1)} %all-gather.2.cloned.1.call-done), kind=kOutput, calls=%fused_computation.1 | convolution fusion | flops 2147483648 | bytes 9437184 | tf_op jit(solution)/shard_map/ipm,ipn->mn/dot_general | solution.py:27
  102.5 0.0 copy-start.1
  102.5 0.0 copy-start.2
  102.5 0.0 copy-start.3
  102.5 0.0 reduce-scatter.2.cloned.1.call-update
  102.6 1.2 copy-done.1
  103.8 0.0 copy-done.2
  103.8 0.4 fusion.3
  104.1 0.0 copy-done.3
  104.1 0.3 fusion.2
  104.4 16.3 %psum.14 = f32[64,128]{1,0:T(8,128)S(1)} all-reduce(f32[64,128]{1,0:T(8,128)S(1)} %fusion.2), channel_id=1, replica_groups=mesh['occ'=8,'ao'=4] {'ao'}, use_global_device_ids=true, to_apply=%region_1.2 | all-reduce | flops 8192 | bytes 65536 | tf_op jit(solution)/shard_map/psum | solution.py:25
  120.7 23.8 %psum.15 = f32[8192]{0:T(1024)} all-reduce(f32[8192]{0:T(1024)S(1)} %bitcast.25), channel_id=1, replica_groups=mesh['occ'=8,'ao'=4] {'occ'}, use_global_device_ids=true, to_apply=%region_2.3 | all-reduce | flops 8192 | bytes 65536 | tf_op jit(solution)/shard_map/psum | solution.py:25
  144.6 8.1 %reduce-scatter.2.cloned.1.call-done = f32[512,256]{1,0:T(8,128)} async-done(((f32[512,2048]{1,0:T(8,128)}), f32[512,256]{1,0:T(8,128)}) %reduce-scatter.2.cloned.1.call-update) | async-done | bytes 524304 | tf_op jit(solution)/shard_map/reduce_scatter | solution.py:33
  (2 shorter events, 0.0 us)
Async XLA Ops:
  7.2 1.6 %copy-start = (bf16[64,128,128]{2,1,0:T(8,128)(2,1)S(1)}, bf16[64,128,128]{2,1,0:T(8,128)(2,1)}, u32[]{:S(2)}) copy-start(bf16[64,128,128]{2,1,0:T(8,128)(2,1)} %param.7) | copy-start | bytes 6291460
  7.2 88.5 %all-gather.2.cloned.1.call-start = ((), (), s32[]{:S(2)}) async-start(), calls=%async_computation.1 | async-start | bytes 5242880 | tf_op jit(solution)/shard_map/all_gather | solution.py:30
  12.1 140.6 %reduce-scatter.2.cloned.1.call-start = ((), (), s32[]{:S(2)}) async-start(), calls=%async_computation.2 | async-start | bytes 4718592 | tf_op jit(solution)/shard_map/reduce_scatter | solution.py:33
  102.5 1.2 copy-start.1
  102.5 1.2 copy-start.2
  102.5 1.6 copy-start.3
Sparse Core Ops, SparseCore 0:
  12.2 83.4 all-gather.1
  102.7 49.9 reduce-scatter.1
